TPU v7x, 128 devices: a whole 4x4x4 slice. The times are simulated.
128 devices in a mesh: group: 4 (over y_hi, core), member: 32 (over x, y_lo, z).
Axes of the slice: x: 4, y: 4 (y_hi: 2, y_lo: 2; y = y_hi * 2 + y_lo), z: 4, core: 2. Of those that a mesh axis runs over, the one named last changes fastest.
Arguments:
- face_schur: float32 [512, 6, 256, 256], P(('group', 'member')), as said below
- face_inverse: float32 [512, 6, 256, 256], P(('group', 'member')), as said below
- face_basis: float32 [512, 6, 96, 256], P(('group', 'member')), may hold values from -6 to 6
- partner: int32 [512, 6], P(('group', 'member')), may hold values from 0 to 3071, as said below
- prim_index: int32 [512, 96], P(('group', 'member')), may hold values from 0 to 24575
Outputs:
- deluxe_basis: float32 [512, 6, 96, 256], P(('group', 'member'))
- coarse_blocks: float32 [512, 9216], P('group')
Inputs may be any that keep to these rules, and one draw needn't show every extreme that they name: partner pairs the faces: the partner of the partner of a face is the face itself; a face of subdomain s has its partner on another device of the same group, where subdomain s lies on device s // 4 and devices k * 32 to (k + 1) * 32 - 1 form group k; at most 1 faces of one device have partners on one other device, and some pair of devices has exactly 1. Every block of face_schur is exactly symmetric and positive definite. Every block of face_inverse is exactly symmetric.
All inputs are finite; a program needn't handle non-finite values.
Results may differ from a plain program's by a relative error of at most 0.0003.
Values sent between devices are 32-bit elements; how exact they have to be, the bound alone decides.
No kernel may reach another device: no remote copies, remote signals or barrier semaphores. Data moves between devices by JAX's collectives and lax.ppermute only.
A program may use at most 128 MiB of HBM per device.

v0:
```python
import jax
import jax.numpy as jnp
from jax import lax
from jax.sharding import PartitionSpec as P

SWEEPS = 2
COARSE_PER_SUB = 48
FULL_PRECISION = lax.Precision.HIGHEST


def inverse_sweeps(summed, initial):
    doubled = 2.0 * jnp.eye(summed.shape[-1], dtype=jnp.float32)
    current = initial
    for repeat in range(SWEEPS):
        applied = jnp.einsum("fij,fjk->fik", summed, current, precision=FULL_PRECISION)
        current = jnp.einsum("fij,fjk->fik", current, doubled - applied, precision=FULL_PRECISION)
    return current


def face_terms(own_schur, other_schur, own_inverse, other_inverse, basis):
    summed = own_schur + other_schur
    approx_inverse = inverse_sweeps(summed, 0.25 * (own_inverse + other_inverse))
    product = jnp.einsum("fck,fjk->fcj", basis, own_schur, precision=FULL_PRECISION)
    deluxe = jnp.einsum("fck,fik->fci", product, approx_inverse, precision=FULL_PRECISION)
    weighted = jnp.einsum("fci,fij->fcj", deluxe, other_schur, precision=FULL_PRECISION)
    face_block = jnp.einsum("fcj,fdj->fcd", weighted, deluxe, precision=FULL_PRECISION)
    return (deluxe, face_block)


def assemble_diagonal(local_diagonal):
    return lax.psum(local_diagonal, ("group", "member"))


def local(face_schur, face_inverse, face_basis, partner, prim_index):
    sub_count = face_schur.shape[0]
    face_width = face_schur.shape[-1]
    prim_count = face_basis.shape[2]
    face_count = sub_count * 6
    members = lax.axis_size("member")
    groups = lax.axis_size("group")
    capacity = (face_count + members - 2) // (members - 1)
    own_schur = face_schur.reshape(face_count, face_width, face_width)
    own_inverse = face_inverse.reshape(face_count, face_width, face_width)
    basis = face_basis.reshape(face_count, prim_count, face_width)
    targets = partner.reshape(face_count)
    target_member = targets // face_count % members
    target_local = targets % face_count
    same_peer = target_member[:, None] == target_member[None, :]
    order_index = jnp.arange(face_count, dtype=jnp.int32)
    send_rank = jnp.sum(same_peer & (order_index[None, :] < order_index[:, None]), axis=1)
    recv_rank = jnp.sum(same_peer & (target_local[None, :] < target_local[:, None]), axis=1)
    stacked = jnp.stack([own_schur, own_inverse], axis=1)
    buffer = (
        jnp.zeros((members, capacity) + stacked.shape[1:], jnp.float32)
        .at[target_member, send_rank]
        .set(stacked)
    )
    received = lax.all_to_all(buffer, "member", split_axis=0, concat_axis=0, tiled=True)
    picked = received[target_member, recv_rank]
    deluxe, face_block = face_terms(own_schur, picked[:, 0], own_inverse, picked[:, 1], basis)
    galerkin = jnp.sum(face_block.reshape(sub_count, 6, prim_count, prim_count), axis=1)
    diagonal_terms = jnp.diagonal(galerkin, axis1=1, axis2=2)
    coarse_total = COARSE_PER_SUB * sub_count * groups * members
    local_diagonal = (
        jnp.zeros((coarse_total,), jnp.float32)
        .at[prim_index.reshape(-1)]
        .add(diagonal_terms.reshape(-1))
    )
    assembled = assemble_diagonal(local_diagonal)
    scales = 1.0 / jnp.sqrt(assembled[prim_index])
    scaled = scales[:, :, None] * galerkin * scales[:, None, :]
    coarse_blocks = lax.all_gather(
        scaled.reshape(sub_count, prim_count * prim_count), "member", axis=0, tiled=True
    )
    deluxe_basis = deluxe.reshape(sub_count, 6, prim_count, face_width)
    return (deluxe_basis, coarse_blocks)


def solution(mesh):
    in_specs = (
        P(("group", "member"), None, None, None),
        P(("group", "member"), None, None, None),
        P(("group", "member"), None, None, None),
        P(("group", "member"), None),
        P(("group", "member"), None),
    )
    out_specs = (P(("group", "member"), None, None, None), P("group", None))
    return jax.shard_map(local, mesh=mesh, in_specs=in_specs, out_specs=out_specs, check_vma=False)
```

profile of v0, /device:TPU:0, one launch (start us, length us, event | category | flops | bytes accessed | tf_op | source)
XLA Modules:
  0.0 763.6 jit_solution(1772734053315307162)
XLA Ops:
  7.2 0.8 broadcast_divide_fusion
  8.0 0.7 compare_and_fusion.2
  9.2 0.2 convert_reduce_fusion
  9.4 10.6 %pad_maximum_fusion = f32[24,2,256,256]{3,2,1,0:T(8,128)} fusion(f32[24,1,256,256]{3,2,1,0:T(8,128)} %bitcast.62, f32[24,1,256,256]{3,2,1,0:T(8,128)} %bitcast.58), kind=kLoop, calls=%fused_computation.5 | loop fusion | flops 3145728 | bytes 25165824 | tf_op jit(solution)/shard_map/stack | solution.py:52
  20.0 7.8 %broadcast.301 = f32[32,2,256,256]{3,2,1,0:T(8,128)} broadcast(f32[]{:T(128)} %constant.47.clone.1), dimensions={} | broadcast | bytes 16777220 | tf_op jit(solution)/shard_map/broadcast_in_dim | solution.py:54
  27.7 23.2 %scatter_fusion = f32[32,2,256,256]{3,2,1,0:T(8,128)} fusion(f32[32,2,256,256]{3,2,1,0:T(8,128)} %broadcast.301, s32[24]{0:T(128)S(1)} %fusion.24, f32[24,2,256,256]{3,2,1,0:T(8,128)} %pad_maximum_fusion), kind=kCustom, calls=%fused_computation.3 | custom fusion | bytes 37748832 | tf_op jit(solution)/shard_map/scatter | solution.py:56
  50.9 9.3 %all-to-all-start = ((f32[32,1,2,256,256]{4,3,2,1,0:T(8,128)}), f32[32,1,2,256,256]{4,3,2,1,0:T(8,128)}, u32[]{:S(2)}, u32[]{:S(2)}) async-start(f32[32,1,2,256,256]{4,3,2,1,0:T(8,128)} %bitcast.57), calls=%async_computation | async-start | bytes 33554432 | tf_op jit(solution)/shard_map/all_to_all | solution.py:58
  60.3 0.1 reshape.273
  60.5 10.1 %fusion.25 = f32[24,96,256]{2,1,0:T(8,128)} fusion(f32[24,96,256]{2,1,0:T(8,128)S(1)} %bitcast.56, f32[24,256,256]{2,1,0:T(8,128)} %bitcast.59), kind=kOutput, calls=%fused_computation.59 | convolution fusion | flops 1811939328 | bytes 11010048 | tf_op jit(solution)/shard_map/fck,fjk->fcj/dot_general | solution.py:23
  70.6 262.5 %all-to-all-done = f32[32,1,2,256,256]{4,3,2,1,0:T(8,128)} async-done(((f32[32,1,2,256,256]{4,3,2,1,0:T(8,128)}), f32[32,1,2,256,256]{4,3,2,1,0:T(8,128)}, u32[]{:S(2)}, u32[]{:S(2)}) %all-to-all-start) | async-done | bytes 16777248 | tf_op jit(solution)/shard_map/all_to_all | solution.py:58
  333.0 13.5 %gather_fusion = f32[24,2,256,256]{3,2,1,0:T(8,128)} fusion(f32[32,1,2,256,256]{4,3,2,1,0:T(8,128)} %all-to-all-done, s32[24]{0:T(128)S(1)} %get-tuple-element.4), kind=kCustom, calls=%fused_computation | custom fusion | bytes 25166016 | tf_op jit(solution)/shard_map/gather | solution.py:59
  346.5 9.0 %fusion.1 = f32[24,256,256]{2,1,0:T(8,128)} fusion(f32[24,2,256,256]{3,2,1,0:T(8,128)} %gather_fusion, f32[4,6,256,256]{3,2,1,0:T(8,128)} %param.6), kind=kLoop, calls=%fused_computation.9 | loop fusion | flops 3145728 | bytes 18874368 | tf_op jit(solution)/shard_map/mul | solution.py:22
  355.5 1.4 copy-done.2
  357.0 13.8 %fusion.12 = f32[24,256,256]{2,1,0:T(8,128)} fusion(f32[24,256,256]{2,1,0:T(8,128)} %fusion.1, f32[24,256,256]{2,1,0:T(8,128)} %bitcast.60, f32[24,2,256,256]{3,2,1,0:T(8,128)S(1)} %copy-done.2), kind=kOutput, calls=%fused_computation.19 | convolution fusion | flops 4833411072 | bytes 25165824 | tf_op jit(solution)/shard_map/fij,fjk->fik/dot_general | solution.py:15
  370.7 14.0 %fusion.4 = f32[24,256,256]{2,1,0:T(8,128)} fusion(f32[24,256,256]{2,1,0:T(8,128)} %fusion.1, f32[24,256,256]{2,1,0:T(8,128)} %fusion.12, f32[256,256]{1,0:T(8,128)S(1)} %fusion.14), kind=kOutput, calls=%fused_computation.12 | convolution fusion | flops 4833411072 | bytes 19136512 | tf_op jit(solution)/shard_map/fij,fjk->fik/dot_general | solution.py:16
  384.8 14.0 %fusion.10 = f32[24,256,256]{2,1,0:T(8,128)} fusion(f32[24,256,256]{2,1,0:T(8,128)} %fusion.4, f32[24,256,256]{2,1,0:T(8,128)} %bitcast.61, f32[24,2,256,256]{3,2,1,0:T(8,128)S(1)} %copy-done.2), kind=kOutput, calls=%fused_computation.18 | convolution fusion | flops 4833411072 | bytes 25165824 | tf_op jit(solution)/shard_map/fij,fjk->fik/dot_general | solution.py:15
  398.8 12.8 %fusion.2 = f32[24,256,256]{2,1,0:T(8,128)S(1)} fusion(f32[24,256,256]{2,1,0:T(8,128)} %fusion.4, f32[24,256,256]{2,1,0:T(8,128)} %fusion.10, f32[256,256]{1,0:T(8,128)S(1)} %fusion.14), kind=kOutput, calls=%fused_computation.10 | convolution fusion | flops 4833411072 | bytes 19136512 | tf_op jit(solution)/shard_map/fij,fjk->fik/dot_general | solution.py:16
  411.6 5.9 fusion.26
  417.5 4.2 fusion.6
  421.7 2.4 fusion.27
  424.2 0.1 reduce_sum.35
  424.3 3.2 copy.25
  427.5 2.9 gather_fusion.1
  430.5 0.1 reshape.293
  430.6 3.9 scatter_custom_fusion.1
  434.6 154.5 %all-reduce.2.cloned.1.call-done = f32[24576]{0:T(1024)} async-done(((f32[24576]{0:T(1024)}), f32[24576]{0:T(1024)}) %all-reduce.2.cloned.1.call-update) | async-done | bytes 98320 | tf_op jit(solution)/shard_map/psum | solution.py:31
  589.1 3.6 gather_fusion.2
  592.7 0.1 reshape.299
  592.8 1.1 multiply_multiply_fusion
  593.8 0.8 reshape.300
  594.7 156.2 %all-gather.3.cloned.1.call-done = f32[32,4,9216]{2,1,0:T(4,128)} async-done(((f32[1,4,9216]{2,1,0:T(4,128)}), f32[32,4,9216]{2,1,0:T(4,128)}) %all-gather.3.cloned.1.call-update) | async-done | bytes 4718608 | tf_op jit(solution)/shard_map/all_gather | solution.py:72
  750.9 5.6 reshape.301
  (33 shorter events, 0.8 us)
Async XLA Ops:
  7.2 53.3 %copy-start = (f32[4,6,96,256]{3,2,1,0:T(8,128)S(1)}, f32[4,6,96,256]{3,2,1,0:T(8,128)}, u32[]{:S(2)}) copy-start(f32[4,6,96,256]{3,2,1,0:T(8,128)} %param.7) | copy-start | bytes 7077892
  50.9 9.3 %copy-start.6 = (s32[4,96]{1,0:T(4,128)S(1)}, s32[4,96]{1,0:T(4,128)}, u32[]{:S(2)}) copy-start(s32[4,96]{1,0:T(4,128)} %param.9) | copy-start | bytes 4612
  50.9 282.1 %all-to-all-start = ((f32[32,1,2,256,256]{4,3,2,1,0:T(8,128)}), f32[32,1,2,256,256]{4,3,2,1,0:T(8,128)}, u32[]{:S(2)}, u32[]{:S(2)}) async-start(f32[32,1,2,256,256]{4,3,2,1,0:T(8,128)} %bitcast.57), calls=%async_computation | async-start | bytes 33554432 | tf_op jit(solution)/shard_map/all_to_all | solution.py:58
  60.2 528.9 %all-reduce.2.cloned.1.call-start = ((), (), s32[]{:S(2)}) async-start(), calls=%async_computation.1 | async-start | bytes 196608 | tf_op jit(solution)/shard_map/psum | solution.py:31
  346.5 10.5 %copy-start.2 = (f32[24,2,256,256]{3,2,1,0:T(8,128)S(1)}, f32[24,2,256,256]{3,2,1,0:T(8,128)}, u32[]{:S(2)}) copy-start(f32[24,2,256,256]{3,2,1,0:T(8,128)} %gather_fusion) | copy-start | bytes 37748740
  398.8 12.8 %copy-start.4 = (f32[24,96,256]{2,1,0:T(8,128)S(1)}, f32[24,96,256]{2,1,0:T(8,128)}, u32[]{:S(2)}) copy-start(f32[24,96,256]{2,1,0:T(8,128)} %fusion.25) | copy-start | bytes 7077892
  417.5 6.7 copy-start.3
  424.3 6.1 copy-start.5
  430.6 325.9 %copy-start.1 = (f32[4,6,96,256]{3,2,1,0:T(8,128)S(1)}, f32[4,6,96,256]{3,2,1,0:T(8,128)}, u32[]{:S(2)}) copy-start(f32[4,6,96,256]{3,2,1,0:T(8,128)} %param.7) | copy-start | bytes 7077892
  434.5 316.3 %all-gather.3.cloned.1.call-start = ((), (), s32[]{:S(2)}) async-start(), calls=%async_computation.2 | async-start | bytes 4866048 | tf_op jit(solution)/shard_map/all_gather | solution.py:72
Sparse Core Ops, SparseCore 0:
  434.6 154.4 all-reduce.1
  594.8 155.9 all-gather.2
where the time goes:
time: 770 us; the launch traced here: 764 us
  waiting for transfers between devices  573 us (74%)
  matrix products  77.3 us (10%)
  local copies, waits for them, and re-layouts  62.8 us (8%)
  other arithmetic  26.5 us (3%)
  between operations  14.5 us (2%)
  starting transfers between devices  9.35 us (1%)
    all_to_all x1, waiting for transfers between devices, local(): lax.all_to_all(buffer, 'member', split_axis=0, concat_axis=0, tiled=True)  262 us
    all_gather x1, waiting for transfers between devices, local(): lax.all_gather(scaled.reshape(sub_count, prim_count * prim_count), 'membe...  156 us
    psum x1, waiting for transfers between devices, assemble_diagonal(): return lax.psum(local_diagonal, ('group', 'member'))  155 us
    dot_general x2, matrix products, inverse_sweeps(): jnp.einsum('fij,fjk->fik', summed, current, precision=FULL_PRECISION)  27.8 us
    dot_general x2, matrix products, inverse_sweeps(): jnp.einsum('fij,fjk->fik', current, doubled - applied, precision=FULL_PRE...  26.8 us
    scatter x1, local copies, waits for them, and re-layouts, local(): buffer = jnp.zeros((members, capacity) + stacked.shape[1:], jnp.float32)....  23.2 us
  transfers between devices with their start and end apart: 3, of which 3 were waited for; matrix products, arithmetic and copies ran while one was open for 1% of the time, Pallas kernels for 0%

commit v1 on v0

--- a/solution.py
+++ b/solution.py
@@ -28,7 +28,7 @@
 
 
 def assemble_diagonal(local_diagonal):
-    return lax.psum(local_diagonal, ("group", "member"))
+    return jnp.sum(lax.all_gather(local_diagonal, ("group", "member")), axis=0)
 
 
 def local(face_schur, face_inverse, face_basis, partner, prim_index):

time: 770 us -> 962 us (1.25)
  waiting for transfers between devices: 573 us -> 750 us
  local copies, waits for them, and re-layouts: 62.8 us -> 73.7 us
    all_gather x0 -> x1, waiting for transfers between devices: none -> 328 us  [assemble_diagonal(): return jnp.sum(lax.all_gather(local_diagonal, ('group', 'member')), axis=0)]
    psum x1 -> x0, waiting for transfers between devices: 155 us -> none  [assemble_diagonal(): return lax.psum(local_diagonal, ('group', 'member'))]
    all_gather x0 -> x1, local copies, waits for them, and re-layouts: none -> 11.9 us  [assemble_diagonal(): return jnp.sum(lax.all_gather(local_diagonal, ('group', 'member')), axis=0)]
where the time goes in v1:
time: 962 us; the launch traced here: 956 us
  waiting for transfers between devices  750 us (78%)
  matrix products  77.2 us (8%)
  local copies, waits for them, and re-layouts  73.7 us (8%)
  other arithmetic  31 us (3%)
  between operations  14.5 us (2%)
    all_gather x1, waiting for transfers between devices, assemble_diagonal(): return jnp.sum(lax.all_gather(local_diagonal, ('group', 'member')), axis=0)  328 us
    all_to_all x1, waiting for transfers between devices, local(): lax.all_to_all(buffer, 'member', split_axis=0, concat_axis=0, tiled=True)  262 us
    all_gather x1, waiting for transfers between devices, local(): lax.all_gather(scaled.reshape(sub_count, prim_count * prim_count), 'membe...  159 us
    dot_general x2, matrix products, inverse_sweeps(): jnp.einsum('fij,fjk->fik', summed, current, precision=FULL_PRECISION)  27.7 us
    dot_general x2, matrix products, inverse_sweeps(): jnp.einsum('fij,fjk->fik', current, doubled - applied, precision=FULL_PRE...  26.8 us
    scatter x1, local copies, waits for them, and re-layouts, local(): buffer = jnp.zeros((members, capacity) + stacked.shape[1:], jnp.float32)....  23.1 us
  transfers between devices with their start and end apart: 3, of which 3 were waited for; matrix products, arithmetic and copies ran while one was open for 1% of the time, Pallas kernels for 0%

profile of v1, /device:TPU:0, one launch (start us, length us, event | category | flops | bytes accessed | tf_op | source)
XLA Modules:
  0.0 955.8 jit_solution(4781393988797050674)
XLA Ops:
  7.2 0.8 broadcast_divide_fusion
  8.0 0.7 compare_and_fusion.2
  9.2 0.2 convert_reduce_fusion
  9.4 10.6 %pad_maximum_fusion = f32[24,2,256,256]{3,2,1,0:T(8,128)} fusion(f32[24,1,256,256]{3,2,1,0:T(8,128)} %bitcast.62, f32[24,1,256,256]{3,2,1,0:T(8,128)} %bitcast.58), kind=kLoop, calls=%fused_computation.5 | loop fusion | flops 3145728 | bytes 25165824 | tf_op jit(solution)/shard_map/stack | solution.py:52
  20.0 7.8 broadcast.301
  27.7 23.1 %scatter_fusion = f32[32,2,256,256]{3,2,1,0:T(8,128)} fusion(f32[32,2,256,256]{3,2,1,0:T(8,128)} %broadcast.301, s32[24]{0:T(128)S(1)} %fusion.24, f32[24,2,256,256]{3,2,1,0:T(8,128)} %pad_maximum_fusion), kind=kCustom, calls=%fused_computation.3 | custom fusion | bytes 37748832 | tf_op jit(solution)/shard_map/scatter | solution.py:56
  50.8 9.3 all-to-all-start
  60.3 10.1 %fusion.25 = f32[24,96,256]{2,1,0:T(8,128)} fusion(f32[24,96,256]{2,1,0:T(8,128)S(1)} %bitcast.56, f32[24,256,256]{2,1,0:T(8,128)} %bitcast.59), kind=kOutput, calls=%fused_computation.59 | convolution fusion | flops 1811939328 | bytes 11010048 | tf_op jit(solution)/shard_map/fck,fjk->fcj/dot_general | solution.py:23
  70.4 262.5 %all-to-all-done = f32[32,1,2,256,256]{4,3,2,1,0:T(8,128)} async-done(((f32[32,1,2,256,256]{4,3,2,1,0:T(8,128)}), f32[32,1,2,256,256]{4,3,2,1,0:T(8,128)}, u32[]{:S(2)}, u32[]{:S(2)}) %all-to-all-start) | async-done | bytes 16777248 | tf_op jit(solution)/shard_map/all_to_all | solution.py:58
  332.9 13.5 %gather_fusion = f32[24,2,256,256]{3,2,1,0:T(8,128)} fusion(f32[32,1,2,256,256]{4,3,2,1,0:T(8,128)} %all-to-all-done, s32[24]{0:T(128)S(1)} %get-tuple-element.4), kind=kCustom, calls=%fused_computation | custom fusion | bytes 25166016 | tf_op jit(solution)/shard_map/gather | solution.py:59
  346.3 9.0 fusion.1
  355.4 1.4 copy-done.2
  356.8 13.8 %fusion.12 = f32[24,256,256]{2,1,0:T(8,128)} fusion(f32[24,256,256]{2,1,0:T(8,128)} %fusion.1, f32[24,256,256]{2,1,0:T(8,128)} %bitcast.60, f32[24,2,256,256]{3,2,1,0:T(8,128)S(1)} %copy-done.2), kind=kOutput, calls=%fused_computation.19 | convolution fusion | flops 4833411072 | bytes 25165824 | tf_op jit(solution)/shard_map/fij,fjk->fik/dot_general | solution.py:15
  370.5 14.0 %fusion.4 = f32[24,256,256]{2,1,0:T(8,128)} fusion(f32[24,256,256]{2,1,0:T(8,128)} %fusion.1, f32[24,256,256]{2,1,0:T(8,128)} %fusion.12, f32[256,256]{1,0:T(8,128)S(1)} %fusion.14), kind=kOutput, calls=%fused_computation.12 | convolution fusion | flops 4833411072 | bytes 19136512 | tf_op jit(solution)/shard_map/fij,fjk->fik/dot_general | solution.py:16
  384.6 13.9 %fusion.10 = f32[24,256,256]{2,1,0:T(8,128)} fusion(f32[24,256,256]{2,1,0:T(8,128)} %fusion.4, f32[24,256,256]{2,1,0:T(8,128)} %bitcast.61, f32[24,2,256,256]{3,2,1,0:T(8,128)S(1)} %copy-done.2), kind=kOutput, calls=%fused_computation.18 | convolution fusion | flops 4833411072 | bytes 25165824 | tf_op jit(solution)/shard_map/fij,fjk->fik/dot_general | solution.py:15
  398.5 12.8 %fusion.2 = f32[24,256,256]{2,1,0:T(8,128)S(1)} fusion(f32[24,256,256]{2,1,0:T(8,128)} %fusion.4, f32[24,256,256]{2,1,0:T(8,128)} %fusion.10, f32[256,256]{1,0:T(8,128)S(1)} %fusion.14), kind=kOutput, calls=%fused_computation.10 | convolution fusion | flops 4833411072 | bytes 19136512 | tf_op jit(solution)/shard_map/fij,fjk->fik/dot_general | solution.py:16
  411.3 5.9 fusion.26
  417.2 4.2 fusion.6
  421.5 2.4 fusion.27
  423.9 0.1 reduce_sum.44
  424.0 3.2 copy.25
  427.2 2.9 gather_fusion.1
  430.2 0.1 reshape.293
  430.3 3.9 scatter_custom_fusion.1
  434.4 328.4 %all-gather.5.cloned.1.call-done = f32[3145728]{0:T(1024)} async-done(((f32[24576]{0:T(1024)}), f32[3145728]{0:T(1024)}) %all-gather.5.cloned.1.call-update) | async-done | bytes 12582928 | tf_op jit(solution)/shard_map/all_gather | solution.py:31
  762.7 11.9 %reshape.297 = f32[128,24576]{1,0:T(8,128)} reshape(f32[3145728]{0:T(1024)} %all-gather.5.cloned.1.call-done) | data formatting | bytes 25165824 | tf_op jit(solution)/shard_map/all_gather | solution.py:31
  774.7 5.4 reduce_sum.45
  780.1 2.5 gather_fusion.2
  782.8 0.1 multiply_multiply_fusion
  782.9 0.8 reshape.301
  783.8 159.3 %all-gather.7.cloned.1.call-done = f32[32,4,9216]{2,1,0:T(4,128)} async-done(((f32[1,4,9216]{2,1,0:T(4,128)}), f32[32,4,9216]{2,1,0:T(4,128)}) %all-gather.7.cloned.1.call-update) | async-done | bytes 4718608 | tf_op jit(solution)/shard_map/all_gather | solution.py:72
  943.1 5.6 reshape.302
  (37 shorter events, 1.0 us)
Async XLA Ops:
  7.2 53.1 %copy-start = (f32[4,6,96,256]{3,2,1,0:T(8,128)S(1)}, f32[4,6,96,256]{3,2,1,0:T(8,128)}, u32[]{:S(2)}) copy-start(f32[4,6,96,256]{3,2,1,0:T(8,128)} %param.7) | copy-start | bytes 7077892
  50.8 9.3 copy-start.7
  50.8 282.0 %all-to-all-start = ((f32[32,1,2,256,256]{4,3,2,1,0:T(8,128)}), f32[32,1,2,256,256]{4,3,2,1,0:T(8,128)}, u32[]{:S(2)}, u32[]{:S(2)}) async-start(f32[32,1,2,256,256]{4,3,2,1,0:T(8,128)} %bitcast.57), calls=%async_computation | async-start | bytes 33554432 | tf_op jit(solution)/shard_map/all_to_all | solution.py:58
  60.1 702.6 %all-gather.5.cloned.1.call-start = ((), (), s32[]{:S(2)}) async-start(), calls=%async_computation.1 | async-start | bytes 12681216 | tf_op jit(solution)/shard_map/all_gather | solution.py:31
  346.3 10.5 %copy-start.2 = (f32[24,2,256,256]{3,2,1,0:T(8,128)S(1)}, f32[24,2,256,256]{3,2,1,0:T(8,128)}, u32[]{:S(2)}) copy-start(f32[24,2,256,256]{3,2,1,0:T(8,128)} %gather_fusion) | copy-start | bytes 37748740
  398.5 12.8 %copy-start.4 = (f32[24,96,256]{2,1,0:T(8,128)S(1)}, f32[24,96,256]{2,1,0:T(8,128)}, u32[]{:S(2)}) copy-start(f32[24,96,256]{2,1,0:T(8,128)} %fusion.25) | copy-start | bytes 7077892
  417.2 6.7 copy-start.3
  424.0 338.7 %copy-start.5 = (f32[4,96,96]{2,1,0:T(8,128)}, f32[4,96,96]{2,1,0:T(8,128)S(1)}, u32[]{:S(2)}) copy-start(f32[4,96,96]{2,1,0:T(8,128)S(1)} %reduce_sum.44) | copy-start | bytes 442372
  434.2 508.9 %all-gather.7.cloned.1.call-start = ((), (), s32[]{:S(2)}) async-start(), calls=%async_computation.2 | async-start | bytes 4866048 | tf_op jit(solution)/shard_map/all_gather | solution.py:72
  774.7 8.1 copy-start.6
  774.7 174.0 %copy-start.1 = (f32[4,6,96,256]{3,2,1,0:T(8,128)S(1)}, f32[4,6,96,256]{3,2,1,0:T(8,128)}, u32[]{:S(2)}) copy-start(f32[4,6,96,256]{3,2,1,0:T(8,128)} %param.7) | copy-start | bytes 7077892
Sparse Core Ops, SparseCore 0:
  434.3 328.3 all-gather.4
  783.9 159.1 all-gather.6
